TPU v7x, 32 devices: a whole 2x2x4 slice. The times are simulated.
32 devices in a mesh: grp: 4 (over x, core), row: 8 (over z, y).
Axes of the slice: x: 2, y: 2, z: 4, core: 2. Of those that a mesh axis runs over, the one named last changes fastest.
Arguments:
- features: bfloat16 [2048, 4096], P('row', 'grp'), may hold values from -0.125 to 0.125
- residual: float32 [2048, 576], P('row'), may hold values from -6 to 6
- precond: float32 [4096, 1024], P('grp'), as said below
Outputs:
- coefs: float32 [4096, 576], P('grp')
- section_resid: float32 [4, 2048, 576], P('grp', 'row')
Inputs may be any that keep to these rules, and one draw needn't show every extreme that they name: Each 1024 x 1024 block of precond is symmetric and positive definite.
All inputs are finite; a program needn't handle non-finite values.
Results may differ from a plain program's by a relative error of at most 0.009.
Values may be sent and summed in bfloat16 or wider, within the bound.
No kernel may reach another device: no remote copies, remote signals or barrier semaphores. Data moves between devices by JAX's collectives and lax.ppermute only.
A program may use at most 64 MiB of HBM per device.

v0:
```python
import jax
import jax.numpy as jnp
from jax import lax
from jax.sharding import PartitionSpec as P


def from_behind(block, axis, distance):
    devices = range(lax.axis_size(axis))
    route = [(i - distance, i) for i in devices if i - distance in devices]
    return lax.ppermute(block, axis, route)


def chain_sweep(features, residual, precond):
    section_index = lax.axis_index("grp")
    section_count = lax.axis_size("grp")
    row_count, target_width = residual.shape
    block_width = features.shape[1]
    panel_count = 3
    panel_width = target_width // panel_count
    step_count = section_count + panel_count - 1

    def correlate(rounded):
        correlation = lax.dot_general(
            features, rounded, (((0,), (0,)), ((), ())), preferred_element_type=jnp.float32
        )
        correlation = lax.psum(correlation, "row")
        return jnp.dot(precond, correlation, precision=lax.Precision.HIGHEST)

    def turn(turn_index, loop_state):
        current, coef_table, resid_table = loop_state
        position = turn_index - section_index
        inside = jnp.logical_and(position >= 0, position < panel_count)
        panel_slot = jnp.clip(position, 0, panel_count - 1) * panel_width
        fresh_panel = lax.dynamic_slice_in_dim(residual, panel_slot, panel_width, 1)
        current = jnp.where(section_index == 0, fresh_panel, current)
        rounded = current.astype(jnp.bfloat16)
        coefficient = correlate(rounded)
        updated = current - jnp.dot(
            features, coefficient.astype(jnp.bfloat16), preferred_element_type=jnp.float32
        )
        old_coef = lax.dynamic_slice_in_dim(coef_table, panel_slot, panel_width, 1)
        coef_table = lax.dynamic_update_slice_in_dim(
            coef_table, jnp.where(inside, coefficient, old_coef), panel_slot, 1
        )
        old_resid = lax.dynamic_slice_in_dim(resid_table, panel_slot, panel_width, 2)
        resid_table = lax.dynamic_update_slice_in_dim(
            resid_table, jnp.where(inside, updated[None], old_resid), panel_slot, 2
        )
        passed = from_behind(updated, "grp", 1)
        return (passed, coef_table, resid_table)

    start_state = (
        jnp.zeros((row_count, panel_width), jnp.float32),
        jnp.zeros((block_width, target_width), jnp.float32),
        jnp.zeros((1, row_count, target_width), jnp.float32),
    )
    final_state = lax.fori_loop(0, step_count, turn, start_state)
    return (final_state[1], final_state[2])


def local(features, residual, precond):
    return chain_sweep(features, residual, precond)


def solution(mesh):
    placed = (P("row", "grp"), P("row", None), P("grp", None))
    return jax.shard_map(
        local,
        mesh=mesh,
        in_specs=placed,
        out_specs=(P("grp", None), P("grp", "row", None)),
        check_vma=False,
    )
```

profile of v0, /device:TPU:1, one launch (start us, length us, event | category | flops | bytes accessed | tf_op | source)
XLA Modules:
  0.0 584.3 jit_solution(12787085232364067102)
XLA Ops:
  7.2 0.9 broadcast_in_dim.19
  8.1 0.3 broadcast_in_dim.18
  8.3 567.7 %while.18 = (s32[]{:T(128)}, f32[256,192]{0,1:T(8,128)S(1)}, f32[1024,576]{0,1:T(8,128)S(1)}, f32[1,256,576]{1,2,0:T(8,128)}, pred[]{:T(512)}, /*index=5*/s32[]{...) while((s32[]{:T(128)}, f32[256,192]{0,1:T(8,128)S(1)}, ...), condition=%wide.region_2.3_spmd, body=%wide.region_0.2_spmd.sunk | while | flops 2618032128 | bytes 20677516 | solution.py:57
  8.4 0.0 all-reduce.2.cloned.1.call-start
  8.4 2.1 convolution_bitcast_fusion.4
  10.5 0.0 all-reduce.2.cloned.1.call-update
  10.5 78.6 %all-reduce.2.cloned.1.call-done = f32[1024,192]{0,1:T(8,128)} async-done(((f32[1024,192]{0,1:T(8,128)}), f32[1024,192]{0,1:T(8,128)}) %all-reduce.2.cloned.1.call-update) | async-done | bytes 786448 | tf_op jit(solution)/shard_map/while/body/eval_jaxpr/psum | solution.py:26
  89.2 6.3 %select_dynamic-update-slice_fusion.2 = (f32[1024,576]{0,1:T(8,128)S(1)}, bf16[1024,192]{0,1:T(8,128)(2,1)S(1)}) fusion(f32[1024,576]{0,1:T(8,128)S(1)} %get-tuple-element.285, s32[]{:T(128)S(6)} %select_n.97, pred[]{:T(512)S(6)} %and.10, f32[1024,192]{0,1:T(8,128)} %all-reduce.2.cloned.1.call-done, f32[1024,1024]{1,0:T(8,128)} %get-tuple-element.306), kind=kOutput, calls=%fused_computation.4.clone.1 | convolution fusion | flops 2416312320 | bytes 6946821 | tf_op jit(solution)/shard_map/while/body/eval_jaxpr/dot_general | solution.py:27
  95.5 1.3 fusion.23
  96.8 0.8 copy-done.3
  97.6 4.8 collective-permute-start
  102.4 2.6 collective-permute-done
  105.0 2.1 convolution_bitcast_fusion.4
  107.1 76.5 %all-reduce.2.cloned.1.call-done = f32[1024,192]{0,1:T(8,128)} async-done(((f32[1024,192]{0,1:T(8,128)}), f32[1024,192]{0,1:T(8,128)}) %all-reduce.2.cloned.1.call-update) | async-done | bytes 786448 | tf_op jit(solution)/shard_map/while/body/eval_jaxpr/psum | solution.py:26
  183.6 6.3 %select_dynamic-update-slice_fusion.2 = (f32[1024,576]{0,1:T(8,128)S(1)}, bf16[1024,192]{0,1:T(8,128)(2,1)S(1)}) fusion(f32[1024,576]{0,1:T(8,128)S(1)} %get-tuple-element.285, s32[]{:T(128)S(6)} %select_n.97, pred[]{:T(512)S(6)} %and.10, f32[1024,192]{0,1:T(8,128)} %all-reduce.2.cloned.1.call-done, f32[1024,1024]{1,0:T(8,128)} %get-tuple-element.306), kind=kOutput, calls=%fused_computation.4.clone.1 | convolution fusion | flops 2416312320 | bytes 6946821 | tf_op jit(solution)/shard_map/while/body/eval_jaxpr/dot_general | solution.py:27
  189.9 1.3 fusion.23
  191.2 0.8 copy-done.3
  192.0 4.8 collective-permute-start
  196.8 2.6 collective-permute-done
  199.4 2.1 convolution_bitcast_fusion.4
  201.5 76.5 %all-reduce.2.cloned.1.call-done = f32[1024,192]{0,1:T(8,128)} async-done(((f32[1024,192]{0,1:T(8,128)}), f32[1024,192]{0,1:T(8,128)}) %all-reduce.2.cloned.1.call-update) | async-done | bytes 786448 | tf_op jit(solution)/shard_map/while/body/eval_jaxpr/psum | solution.py:26
  278.0 6.3 %select_dynamic-update-slice_fusion.2 = (f32[1024,576]{0,1:T(8,128)S(1)}, bf16[1024,192]{0,1:T(8,128)(2,1)S(1)}) fusion(f32[1024,576]{0,1:T(8,128)S(1)} %get-tuple-element.285, s32[]{:T(128)S(6)} %select_n.97, pred[]{:T(512)S(6)} %and.10, f32[1024,192]{0,1:T(8,128)} %all-reduce.2.cloned.1.call-done, f32[1024,1024]{1,0:T(8,128)} %get-tuple-element.306), kind=kOutput, calls=%fused_computation.4.clone.1 | convolution fusion | flops 2416312320 | bytes 6946821 | tf_op jit(solution)/shard_map/while/body/eval_jaxpr/dot_general | solution.py:27
  284.4 1.3 fusion.23
  285.6 0.8 copy-done.3
  286.4 4.8 collective-permute-start
  291.3 2.6 collective-permute-done
  293.9 2.1 convolution_bitcast_fusion.4
  296.0 76.1 %all-reduce.2.cloned.1.call-done = f32[1024,192]{0,1:T(8,128)} async-done(((f32[1024,192]{0,1:T(8,128)}), f32[1024,192]{0,1:T(8,128)}) %all-reduce.2.cloned.1.call-update) | async-done | bytes 786448 | tf_op jit(solution)/shard_map/while/body/eval_jaxpr/psum | solution.py:26
  372.1 6.3 %select_dynamic-update-slice_fusion.2 = (f32[1024,576]{0,1:T(8,128)S(1)}, bf16[1024,192]{0,1:T(8,128)(2,1)S(1)}) fusion(f32[1024,576]{0,1:T(8,128)S(1)} %get-tuple-element.285, s32[]{:T(128)S(6)} %select_n.97, pred[]{:T(512)S(6)} %and.10, f32[1024,192]{0,1:T(8,128)} %all-reduce.2.cloned.1.call-done, f32[1024,1024]{1,0:T(8,128)} %get-tuple-element.306), kind=kOutput, calls=%fused_computation.4.clone.1 | convolution fusion | flops 2416312320 | bytes 6946821 | tf_op jit(solution)/shard_map/while/body/eval_jaxpr/dot_general | solution.py:27
  378.4 1.3 fusion.23
  379.7 0.8 copy-done.3
  380.5 4.8 collective-permute-start
  385.4 2.6 collective-permute-done
  387.9 2.1 convolution_bitcast_fusion.4
  390.1 76.1 %all-reduce.2.cloned.1.call-done = f32[1024,192]{0,1:T(8,128)} async-done(((f32[1024,192]{0,1:T(8,128)}), f32[1024,192]{0,1:T(8,128)}) %all-reduce.2.cloned.1.call-update) | async-done | bytes 786448 | tf_op jit(solution)/shard_map/while/body/eval_jaxpr/psum | solution.py:26
  466.1 6.3 %select_dynamic-update-slice_fusion.2 = (f32[1024,576]{0,1:T(8,128)S(1)}, bf16[1024,192]{0,1:T(8,128)(2,1)S(1)}) fusion(f32[1024,576]{0,1:T(8,128)S(1)} %get-tuple-element.285, s32[]{:T(128)S(6)} %select_n.97, pred[]{:T(512)S(6)} %and.10, f32[1024,192]{0,1:T(8,128)} %all-reduce.2.cloned.1.call-done, f32[1024,1024]{1,0:T(8,128)} %get-tuple-element.306), kind=kOutput, calls=%fused_computation.4.clone.1 | convolution fusion | flops 2416312320 | bytes 6946821 | tf_op jit(solution)/shard_map/while/body/eval_jaxpr/dot_general | solution.py:27
  472.4 1.3 fusion.23
  473.7 0.8 copy-done.3
  474.5 4.8 collective-permute-start
  479.4 2.6 collective-permute-done
  482.0 2.1 convolution_bitcast_fusion.4
  484.1 76.1 %all-reduce.2.cloned.1.call-done = f32[1024,192]{0,1:T(8,128)} async-done(((f32[1024,192]{0,1:T(8,128)}), f32[1024,192]{0,1:T(8,128)}) %all-reduce.2.cloned.1.call-update) | async-done | bytes 786448 | tf_op jit(solution)/shard_map/while/body/eval_jaxpr/psum | solution.py:26
  560.2 6.3 %select_dynamic-update-slice_fusion.2 = (f32[1024,576]{0,1:T(8,128)S(1)}, bf16[1024,192]{0,1:T(8,128)(2,1)S(1)}) fusion(f32[1024,576]{0,1:T(8,128)S(1)} %get-tuple-element.285, s32[]{:T(128)S(6)} %select_n.97, pred[]{:T(512)S(6)} %and.10, f32[1024,192]{0,1:T(8,128)} %all-reduce.2.cloned.1.call-done, f32[1024,1024]{1,0:T(8,128)} %get-tuple-element.306), kind=kOutput, calls=%fused_computation.4.clone.1 | convolution fusion | flops 2416312320 | bytes 6946821 | tf_op jit(solution)/shard_map/while/body/eval_jaxpr/dot_general | solution.py:27
  566.5 1.3 fusion.23
  567.8 0.8 copy-done.3
  568.6 4.8 collective-permute-start
  573.4 2.6 collective-permute-done
  576.0 1.4 copy-done.1
  (32 shorter events, 0.2 us)
Async XLA Ops:
  7.2 1.2 copy-start
  8.4 80.8 %all-reduce.2.cloned.1.call-start = ((), (), s32[]{:S(2)}) async-start(), calls=%async_computation | async-start | bytes 1572864 | tf_op jit(solution)/shard_map/while/body/eval_jaxpr/psum | solution.py:26
  89.2 6.3 %copy-start.2 = (f32[1,256,576]{1,2,0:T(8,128)S(1)}, f32[1,256,576]{1,2,0:T(8,128)}, u32[]{:S(2)}) copy-start(f32[1,256,576]{1,2,0:T(8,128)} %get-tuple-element.286) | copy-start | bytes 1769476 | tf_op jit(solution)/shard_map/while
  96.7 0.8 copy-start.3
  97.6 7.4 %collective-permute-start = (f32[256,192]{0,1:T(8,128)S(1)}, f32[256,192]{0,1:T(8,128)S(1)}, u32[]{:S(2)}, u32[]{:S(2)}) collective-permute-start(f32[256,192]{0,1:T(8,128)S(1)} %get-tuple-element.265), channel_id=1, source_target_pairs={{0,8},{8,16},{16,24},{1,9},{9,17},{17,25},{2,10},{10,18},{18,26},{... | collective-permute-start | bytes 589832 | tf_op jit(solution)/shard_map/while/body/eval_jaxpr/ppermute | solution.py:10
  105.0 78.6 %all-reduce.2.cloned.1.call-start = ((), (), s32[]{:S(2)}) async-start(), calls=%async_computation | async-start | bytes 1572864 | tf_op jit(solution)/shard_map/while/body/eval_jaxpr/psum | solution.py:26
  183.6 6.3 %copy-start.2 = (f32[1,256,576]{1,2,0:T(8,128)S(1)}, f32[1,256,576]{1,2,0:T(8,128)}, u32[]{:S(2)}) copy-start(f32[1,256,576]{1,2,0:T(8,128)} %get-tuple-element.286) | copy-start | bytes 1769476 | tf_op jit(solution)/shard_map/while
  191.2 0.8 copy-start.3
  192.0 7.4 %collective-permute-start = (f32[256,192]{0,1:T(8,128)S(1)}, f32[256,192]{0,1:T(8,128)S(1)}, u32[]{:S(2)}, u32[]{:S(2)}) collective-permute-start(f32[256,192]{0,1:T(8,128)S(1)} %get-tuple-element.265), channel_id=1, source_target_pairs={{0,8},{8,16},{16,24},{1,9},{9,17},{17,25},{2,10},{10,18},{18,26},{... | collective-permute-start | bytes 589832 | tf_op jit(solution)/shard_map/while/body/eval_jaxpr/ppermute | solution.py:10
  199.4 78.6 %all-reduce.2.cloned.1.call-start = ((), (), s32[]{:S(2)}) async-start(), calls=%async_computation | async-start | bytes 1572864 | tf_op jit(solution)/shard_map/while/body/eval_jaxpr/psum | solution.py:26
  278.0 6.3 %copy-start.2 = (f32[1,256,576]{1,2,0:T(8,128)S(1)}, f32[1,256,576]{1,2,0:T(8,128)}, u32[]{:S(2)}) copy-start(f32[1,256,576]{1,2,0:T(8,128)} %get-tuple-element.286) | copy-start | bytes 1769476 | tf_op jit(solution)/shard_map/while
  285.6 0.8 copy-start.3
  286.4 7.4 %collective-permute-start = (f32[256,192]{0,1:T(8,128)S(1)}, f32[256,192]{0,1:T(8,128)S(1)}, u32[]{:S(2)}, u32[]{:S(2)}) collective-permute-start(f32[256,192]{0,1:T(8,128)S(1)} %get-tuple-element.265), channel_id=1, source_target_pairs={{0,8},{8,16},{16,24},{1,9},{9,17},{17,25},{2,10},{10,18},{18,26},{... | collective-permute-start | bytes 589832 | tf_op jit(solution)/shard_map/while/body/eval_jaxpr/ppermute | solution.py:10
  293.9 78.2 %all-reduce.2.cloned.1.call-start = ((), (), s32[]{:S(2)}) async-start(), calls=%async_computation | async-start | bytes 1572864 | tf_op jit(solution)/shard_map/while/body/eval_jaxpr/psum | solution.py:26
  372.1 6.3 %copy-start.2 = (f32[1,256,576]{1,2,0:T(8,128)S(1)}, f32[1,256,576]{1,2,0:T(8,128)}, u32[]{:S(2)}) copy-start(f32[1,256,576]{1,2,0:T(8,128)} %get-tuple-element.286) | copy-start | bytes 1769476 | tf_op jit(solution)/shard_map/while
  379.7 0.8 copy-start.3
  380.5 7.4 %collective-permute-start = (f32[256,192]{0,1:T(8,128)S(1)}, f32[256,192]{0,1:T(8,128)S(1)}, u32[]{:S(2)}, u32[]{:S(2)}) collective-permute-start(f32[256,192]{0,1:T(8,128)S(1)} %get-tuple-element.265), channel_id=1, source_target_pairs={{0,8},{8,16},{16,24},{1,9},{9,17},{17,25},{2,10},{10,18},{18,26},{... | collective-permute-start | bytes 589832 | tf_op jit(solution)/shard_map/while/body/eval_jaxpr/ppermute | solution.py:10
  387.9 78.2 %all-reduce.2.cloned.1.call-start = ((), (), s32[]{:S(2)}) async-start(), calls=%async_computation | async-start | bytes 1572864 | tf_op jit(solution)/shard_map/while/body/eval_jaxpr/psum | solution.py:26
  466.1 6.3 %copy-start.2 = (f32[1,256,576]{1,2,0:T(8,128)S(1)}, f32[1,256,576]{1,2,0:T(8,128)}, u32[]{:S(2)}) copy-start(f32[1,256,576]{1,2,0:T(8,128)} %get-tuple-element.286) | copy-start | bytes 1769476 | tf_op jit(solution)/shard_map/while
  473.7 0.8 copy-start.3
  474.5 7.4 %collective-permute-start = (f32[256,192]{0,1:T(8,128)S(1)}, f32[256,192]{0,1:T(8,128)S(1)}, u32[]{:S(2)}, u32[]{:S(2)}) collective-permute-start(f32[256,192]{0,1:T(8,128)S(1)} %get-tuple-element.265), channel_id=1, source_target_pairs={{0,8},{8,16},{16,24},{1,9},{9,17},{17,25},{2,10},{10,18},{18,26},{... | collective-permute-start | bytes 589832 | tf_op jit(solution)/shard_map/while/body/eval_jaxpr/ppermute | solution.py:10
  482.0 78.2 %all-reduce.2.cloned.1.call-start = ((), (), s32[]{:S(2)}) async-start(), calls=%async_computation | async-start | bytes 1572864 | tf_op jit(solution)/shard_map/while/body/eval_jaxpr/psum | solution.py:26
  560.2 6.3 %copy-start.2 = (f32[1,256,576]{1,2,0:T(8,128)S(1)}, f32[1,256,576]{1,2,0:T(8,128)}, u32[]{:S(2)}) copy-start(f32[1,256,576]{1,2,0:T(8,128)} %get-tuple-element.286) | copy-start | bytes 1769476 | tf_op jit(solution)/shard_map/while
  567.8 0.8 copy-start.3
  568.6 7.4 %collective-permute-start = (f32[256,192]{0,1:T(8,128)S(1)}, f32[256,192]{0,1:T(8,128)S(1)}, u32[]{:S(2)}, u32[]{:S(2)}) collective-permute-start(f32[256,192]{0,1:T(8,128)S(1)} %get-tuple-element.265), channel_id=1, source_target_pairs={{0,8},{8,16},{16,24},{1,9},{9,17},{17,25},{2,10},{10,18},{18,26},{... | collective-permute-start | bytes 589832 | tf_op jit(solution)/shard_map/while/body/eval_jaxpr/ppermute | solution.py:10
  576.0 1.4 copy-start.1
Sparse Core Ops, SparseCore 0:
  13.2 75.9 all-reduce.1
  109.8 73.7 all-reduce.1
  204.2 73.7 all-reduce.1
  298.3 73.7 all-reduce.1
  392.4 73.6 all-reduce.1
  486.4 73.6 all-reduce.1
where the time goes:
time: 585 us; the launch traced here: 584 us
  waiting for transfers between devices  475 us (81%)
  matrix products  57.9 us (10%)
  starting transfers between devices  29 us (5%)
  between operations  14 us (2%)
  local copies, waits for them, and re-layouts  7.44 us (1%)
    psum x6, waiting for transfers between devices, correlate(): correlation = lax.psum(correlation, 'row')  460 us
    dot_general x6, matrix products, correlate(): return jnp.dot(precond, correlation, precision=lax.Precision.HIGHEST)  37.8 us
    ppermute x6, starting transfers between devices, from_behind(): return lax.ppermute(block, axis, route)  29 us
    ppermute x6, waiting for transfers between devices, from_behind(): return lax.ppermute(block, axis, route)  15.5 us
    dot_general x6, matrix products, correlate(): lax.dot_general(features, rounded, (((0,), (0,)), ((), ())), preferred_el...  12.5 us
  transfers between devices with their start and end apart: 12, of which 12 were waited for; matrix products, arithmetic and copies ran while one was open for 0% of the time, Pallas kernels for 0%

commit v1 on v0

--- a/solution.py
+++ b/solution.py
@@ -23,7 +23,8 @@
         correlation = lax.dot_general(
             features, rounded, (((0,), (0,)), ((), ())), preferred_element_type=jnp.float32
         )
-        correlation = lax.psum(correlation, "row")
+        parts = lax.all_gather(correlation, "row")
+        correlation = jnp.sum(parts, axis=0)
         return jnp.dot(precond, correlation, precision=lax.Precision.HIGHEST)
 
     def turn(turn_index, loop_state):

time: 585 us -> 760 us (1.30)
  waiting for transfers between devices: 475 us -> 603 us
  local copies, waits for them, and re-layouts: 7.44 us -> 55 us
  matrix products: 57.9 us -> 47.7 us
  other arithmetic: 0 us -> 9.07 us
    all_gather x0 -> x6, waiting for transfers between devices: none -> 587 us  [correlate(): parts = lax.all_gather(correlation, 'row')]
    psum x6 -> x0, waiting for transfers between devices: 460 us -> none  [correlate(): correlation = lax.psum(correlation, 'row')]
    while x24 -> x30, local copies, waits for them, and re-layouts: 4.88 us -> 53.1 us
    dot_general x6, matrix products: 37.8 us -> 26.3 us  [correlate(): return jnp.dot(precond, correlation, precision=lax.Precision.HIGHEST)]
    reduce_sum x0 -> x6, other arithmetic: none -> 9.07 us  [correlate(): correlation = jnp.sum(parts, axis=0)]
where the time goes in v1:
time: 760 us; the launch traced here: 759 us
  waiting for transfers between devices  603 us (79%)
  local copies, waits for them, and re-layouts  55 us (7%)
  matrix products  47.7 us (6%)
  starting transfers between devices  30.1 us (4%)
  between operations  14 us (2%)
  other arithmetic  9.07 us (1%)
    all_gather x6, waiting for transfers between devices, correlate(): parts = lax.all_gather(correlation, 'row')  587 us
    while x30, local copies, waits for them, and re-layouts  53.1 us
    ppermute x6, starting transfers between devices, from_behind(): return lax.ppermute(block, axis, route)  30 us
    dot_general x6, matrix products, correlate(): return jnp.dot(precond, correlation, precision=lax.Precision.HIGHEST)  26.3 us
    ppermute x6, waiting for transfers between devices, from_behind(): return lax.ppermute(block, axis, route)  15.5 us
  transfers between devices with their start and end apart: 12, of which 12 were waited for; matrix products, arithmetic and copies ran while one was open for 0% of the time, Pallas kernels for 0%

profile of v1, /device:TPU:1, one launch (start us, length us, event | category | flops | bytes accessed | tf_op | source)
XLA Modules:
  0.0 759.3 jit_solution(12378075118462691362)
XLA Ops:
  7.5 743.4 %while.18 = (s32[]{:T(128)}, f32[256,192]{0,1:T(8,128)S(1)}, f32[1024,576]{0,1:T(8,128)S(1)}, f32[1,256,576]{1,2,0:T(8,128)S(1)}, pred[]{:T(512)}, /*index=5*/s3...) while((s32[]{:T(128)}, f32[256,192]{0,1:T(8,128)S(1)}, ...), condition=%wide.region_2.3_spmd, body=%wide.region_0.2_spmd.sunk | while | flops 2619211776 | bytes 71009168 | solution.py:58
  7.6 2.3 convolution_bitcast_fusion.4
  9.9 100.6 %all-gather.5.cloned.1.call-done = f32[8192,192]{0,1:T(8,128)} async-done(((f32[1024,192]{0,1:T(8,128)}), f32[8192,192]{0,1:T(8,128)}) %all-gather.5.cloned.1.call-update) | async-done | bytes 6291472 | tf_op jit(solution)/shard_map/while/body/eval_jaxpr/all_gather | solution.py:26
  110.6 8.2 %copy.7 = f32[24,8,8,1024]{3,2,1,0:T(8,128)S(1)} copy(f32[24,8,8,1024]{3,1,2,0:T(8,128)} %bitcast.40) | data formatting | bytes 12582912 | tf_op jit(solution)/shard_map/while
  118.8 1.5 bitcast_reduce_fusion.2
  120.9 4.4 select_dynamic-update-slice_fusion.2
  125.4 1.3 fusion.23
  126.6 5.0 collective-permute-start
  131.6 2.6 collective-permute-done
  134.2 2.3 convolution_bitcast_fusion.4
  136.6 97.5 %all-gather.5.cloned.1.call-done = f32[8192,192]{0,1:T(8,128)} async-done(((f32[1024,192]{0,1:T(8,128)}), f32[8192,192]{0,1:T(8,128)}) %all-gather.5.cloned.1.call-update) | async-done | bytes 6291472 | tf_op jit(solution)/shard_map/while/body/eval_jaxpr/all_gather | solution.py:26
  234.1 8.2 %copy.7 = f32[24,8,8,1024]{3,2,1,0:T(8,128)S(1)} copy(f32[24,8,8,1024]{3,1,2,0:T(8,128)} %bitcast.40) | data formatting | bytes 12582912 | tf_op jit(solution)/shard_map/while
  242.3 1.5 bitcast_reduce_fusion.2
  244.5 4.4 select_dynamic-update-slice_fusion.2
  248.9 1.3 fusion.23
  250.2 5.0 collective-permute-start
  255.2 2.6 collective-permute-done
  257.8 2.3 convolution_bitcast_fusion.4
  260.1 97.5 %all-gather.5.cloned.1.call-done = f32[8192,192]{0,1:T(8,128)} async-done(((f32[1024,192]{0,1:T(8,128)}), f32[8192,192]{0,1:T(8,128)}) %all-gather.5.cloned.1.call-update) | async-done | bytes 6291472 | tf_op jit(solution)/shard_map/while/body/eval_jaxpr/all_gather | solution.py:26
  357.6 8.2 %copy.7 = f32[24,8,8,1024]{3,2,1,0:T(8,128)S(1)} copy(f32[24,8,8,1024]{3,1,2,0:T(8,128)} %bitcast.40) | data formatting | bytes 12582912 | tf_op jit(solution)/shard_map/while
  365.8 1.5 bitcast_reduce_fusion.2
  368.0 4.4 select_dynamic-update-slice_fusion.2
  372.4 1.3 fusion.23
  373.7 5.0 collective-permute-start
  378.7 2.6 collective-permute-done
  381.3 2.3 convolution_bitcast_fusion.4
  383.6 97.2 %all-gather.5.cloned.1.call-done = f32[8192,192]{0,1:T(8,128)} async-done(((f32[1024,192]{0,1:T(8,128)}), f32[8192,192]{0,1:T(8,128)}) %all-gather.5.cloned.1.call-update) | async-done | bytes 6291472 | tf_op jit(solution)/shard_map/while/body/eval_jaxpr/all_gather | solution.py:26
  480.8 8.2 %copy.7 = f32[24,8,8,1024]{3,2,1,0:T(8,128)S(1)} copy(f32[24,8,8,1024]{3,1,2,0:T(8,128)} %bitcast.40) | data formatting | bytes 12582912 | tf_op jit(solution)/shard_map/while
  489.0 1.5 bitcast_reduce_fusion.2
  491.2 4.4 select_dynamic-update-slice_fusion.2
  496.9 5.0 collective-permute-start
  501.9 2.6 collective-permute-done
  504.5 2.3 convolution_bitcast_fusion.4
  506.8 97.2 %all-gather.5.cloned.1.call-done = f32[8192,192]{0,1:T(8,128)} async-done(((f32[1024,192]{0,1:T(8,128)}), f32[8192,192]{0,1:T(8,128)}) %all-gather.5.cloned.1.call-update) | async-done | bytes 6291472 | tf_op jit(solution)/shard_map/while/body/eval_jaxpr/all_gather | solution.py:26
  604.0 8.2 %copy.7 = f32[24,8,8,1024]{3,2,1,0:T(8,128)S(1)} copy(f32[24,8,8,1024]{3,1,2,0:T(8,128)} %bitcast.40) | data formatting | bytes 12582912 | tf_op jit(solution)/shard_map/while
  612.2 1.5 bitcast_reduce_fusion.2
  614.4 4.4 select_dynamic-update-slice_fusion.2
  620.1 5.0 collective-permute-start
  625.1 2.6 collective-permute-done
  627.7 2.3 convolution_bitcast_fusion.4
  630.0 97.2 %all-gather.5.cloned.1.call-done = f32[8192,192]{0,1:T(8,128)} async-done(((f32[1024,192]{0,1:T(8,128)}), f32[8192,192]{0,1:T(8,128)}) %all-gather.5.cloned.1.call-update) | async-done | bytes 6291472 | tf_op jit(solution)/shard_map/while/body/eval_jaxpr/all_gather | solution.py:26
  727.2 8.2 %copy.7 = f32[24,8,8,1024]{3,2,1,0:T(8,128)S(1)} copy(f32[24,8,8,1024]{3,1,2,0:T(8,128)} %bitcast.40) | data formatting | bytes 12582912 | tf_op jit(solution)/shard_map/while
  735.4 1.5 bitcast_reduce_fusion.2
  737.6 4.4 select_dynamic-update-slice_fusion.2
  742.0 1.3 fusion.23
  743.3 5.0 collective-permute-start
  748.3 2.6 collective-permute-done
  750.9 1.4 copy-done.2
  (44 shorter events, 7.2 us)
Async XLA Ops:
  7.5 103.0 %all-gather.5.cloned.1.call-start = ((), (), s32[]{:S(2)}) async-start(), calls=%async_computation | async-start | bytes 7077888 | tf_op jit(solution)/shard_map/while/body/eval_jaxpr/all_gather | solution.py:26
  118.8 2.2 copy-start
  120.3 5.1 copy-start.1
  126.6 7.6 %collective-permute-start = (f32[256,192]{0,1:T(8,128)S(1)}, f32[256,192]{0,1:T(8,128)S(1)}, u32[]{:S(2)}, u32[]{:S(2)}) collective-permute-start(f32[256,192]{0,1:T(8,128)S(1)} %get-tuple-element.265), channel_id=1, source_target_pairs={{0,8},{8,16},{16,24},{1,9},{9,17},{17,25},{2,10},{10,18},{18,26},{... | collective-permute-start | bytes 589832 | tf_op jit(solution)/shard_map/while/body/eval_jaxpr/ppermute | solution.py:10
  134.2 99.9 %all-gather.5.cloned.1.call-start = ((), (), s32[]{:S(2)}) async-start(), calls=%async_computation | async-start | bytes 7077888 | tf_op jit(solution)/shard_map/while/body/eval_jaxpr/all_gather | solution.py:26
  242.3 2.2 copy-start
  243.8 5.1 copy-start.1
  250.2 7.6 %collective-permute-start = (f32[256,192]{0,1:T(8,128)S(1)}, f32[256,192]{0,1:T(8,128)S(1)}, u32[]{:S(2)}, u32[]{:S(2)}) collective-permute-start(f32[256,192]{0,1:T(8,128)S(1)} %get-tuple-element.265), channel_id=1, source_target_pairs={{0,8},{8,16},{16,24},{1,9},{9,17},{17,25},{2,10},{10,18},{18,26},{... | collective-permute-start | bytes 589832 | tf_op jit(solution)/shard_map/while/body/eval_jaxpr/ppermute | solution.py:10
  257.8 99.9 %all-gather.5.cloned.1.call-start = ((), (), s32[]{:S(2)}) async-start(), calls=%async_computation | async-start | bytes 7077888 | tf_op jit(solution)/shard_map/while/body/eval_jaxpr/all_gather | solution.py:26
  365.8 2.2 copy-start
  367.3 5.1 copy-start.1
  373.7 7.6 %collective-permute-start = (f32[256,192]{0,1:T(8,128)S(1)}, f32[256,192]{0,1:T(8,128)S(1)}, u32[]{:S(2)}, u32[]{:S(2)}) collective-permute-start(f32[256,192]{0,1:T(8,128)S(1)} %get-tuple-element.265), channel_id=1, source_target_pairs={{0,8},{8,16},{16,24},{1,9},{9,17},{17,25},{2,10},{10,18},{18,26},{... | collective-permute-start | bytes 589832 | tf_op jit(solution)/shard_map/while/body/eval_jaxpr/ppermute | solution.py:10
  381.3 99.5 %all-gather.5.cloned.1.call-start = ((), (), s32[]{:S(2)}) async-start(), calls=%async_computation | async-start | bytes 7077888 | tf_op jit(solution)/shard_map/while/body/eval_jaxpr/all_gather | solution.py:26
  489.0 2.2 copy-start
  490.5 5.1 copy-start.1
  496.9 7.6 %collective-permute-start = (f32[256,192]{0,1:T(8,128)S(1)}, f32[256,192]{0,1:T(8,128)S(1)}, u32[]{:S(2)}, u32[]{:S(2)}) collective-permute-start(f32[256,192]{0,1:T(8,128)S(1)} %get-tuple-element.265), channel_id=1, source_target_pairs={{0,8},{8,16},{16,24},{1,9},{9,17},{17,25},{2,10},{10,18},{18,26},{... | collective-permute-start | bytes 589832 | tf_op jit(solution)/shard_map/while/body/eval_jaxpr/ppermute | solution.py:10
  504.5 99.5 %all-gather.5.cloned.1.call-start = ((), (), s32[]{:S(2)}) async-start(), calls=%async_computation | async-start | bytes 7077888 | tf_op jit(solution)/shard_map/while/body/eval_jaxpr/all_gather | solution.py:26
  612.2 2.2 copy-start
  613.8 5.1 copy-start.1
  620.1 7.6 %collective-permute-start = (f32[256,192]{0,1:T(8,128)S(1)}, f32[256,192]{0,1:T(8,128)S(1)}, u32[]{:S(2)}, u32[]{:S(2)}) collective-permute-start(f32[256,192]{0,1:T(8,128)S(1)} %get-tuple-element.265), channel_id=1, source_target_pairs={{0,8},{8,16},{16,24},{1,9},{9,17},{17,25},{2,10},{10,18},{18,26},{... | collective-permute-start | bytes 589832 | tf_op jit(solution)/shard_map/while/body/eval_jaxpr/ppermute | solution.py:10
  627.7 99.5 %all-gather.5.cloned.1.call-start = ((), (), s32[]{:S(2)}) async-start(), calls=%async_computation | async-start | bytes 7077888 | tf_op jit(solution)/shard_map/while/body/eval_jaxpr/all_gather | solution.py:26
  735.4 2.2 copy-start
  737.0 5.1 copy-start.1
  743.3 7.6 %collective-permute-start = (f32[256,192]{0,1:T(8,128)S(1)}, f32[256,192]{0,1:T(8,128)S(1)}, u32[]{:S(2)}, u32[]{:S(2)}) collective-permute-start(f32[256,192]{0,1:T(8,128)S(1)} %get-tuple-element.265), channel_id=1, source_target_pairs={{0,8},{8,16},{16,24},{1,9},{9,17},{17,25},{2,10},{10,18},{18,26},{... | collective-permute-start | bytes 589832 | tf_op jit(solution)/shard_map/while/body/eval_jaxpr/ppermute | solution.py:10
  750.9 1.4 copy-start.2
  750.9 1.6 copy-start.3
Sparse Core Ops, SparseCore 0:
  11.1 99.4 all-gather.4
  137.8 96.2 all-gather.4
  261.3 96.2 all-gather.4
  384.5 96.2 all-gather.4
  507.7 96.2 all-gather.4
  630.9 96.2 all-gather.4
